TPU v7x, 256 devices: a whole 4x4x8 slice. The times are simulated.
256 devices in a mesh: sta: 64 (over x_lo, z, y), tpl: 4 (over x_hi, core).
Axes of the slice: x: 4 (x_hi: 2, x_lo: 2; x = x_hi * 2 + x_lo), y: 4, z: 8, core: 2. Of those that a mesh axis runs over, the one named last changes fastest.
Arguments:
- waveform: float32 [128, 1536], P('sta', 'tpl'), may hold values from -6 to 6
- fir_taps: float32 [64], replicated, may hold values from -0.75 to 0.75
- templates: bfloat16 [512, 128, 1024], P('tpl', 'sta'), may hold values from -6 to 6
- presence: int32 [512, 128], P('tpl', 'sta'), may hold values from 0 to 1
- moveout: int32 [512, 128], P('tpl', 'sta'), may hold values from 0 to 128
Outputs:
- network_stack: float32 [4, 128, 384], P('tpl', 'sta')
All inputs are finite; a program needn't handle non-finite values.
Results may differ from a plain program's by a relative error of at most 0.0029.
Values may be sent and summed in bfloat16 or wider, within the bound.
A program may use at most 64 MiB of HBM per device.

v0:
```python
import jax
import jax.numpy as jnp
from jax import lax
from jax.sharding import PartitionSpec as P

BLK = 128
SHIFT_MOST = 128
epsilon = 1e-06


def fir_apply(extended, coeffs):
    result = lax.conv_general_dilated(
        extended[:, None, :],
        coeffs[::-1][None, None, :],
        (1,),
        "VALID",
        precision=lax.Precision.HIGHEST,
    )
    return result[:, 0, :]


def hankel(samples):
    leading = samples.shape[:-1]
    row_total = samples.shape[-1] // BLK
    row_blocks = samples.reshape(leading + (row_total, BLK))
    windows = jnp.concatenate([row_blocks[..., :-1, :], row_blocks[..., 1:, :]], axis=-1)
    tiled_win = jnp.tile(windows, (1,) * (windows.ndim - 1) + (BLK + 1,))
    flat_win = tiled_win[..., : BLK * (2 * BLK + 1)]
    return flat_win.reshape(windows.shape[:-1] + (BLK, 2 * BLK + 1))[..., :BLK]


def shards(waveform, fir_taps, templates, presence, moveout):
    tap_count = fir_taps.shape[0]
    gathered = lax.all_gather(waveform, "tpl", axis=1, tiled=True)
    extended = jnp.pad(gathered, ((0, 0), (tap_count - 1, 0)))
    filtered = fir_apply(extended, fir_taps).astype(jnp.bfloat16)
    station_count = filtered.shape[0]
    templ_len = templates.shape[2]
    block_rows = templates.shape[0]
    corr_len = filtered.shape[1] - templ_len
    out_len = corr_len - SHIFT_MOST
    time_blocks = corr_len // BLK
    lag_blocks = templ_len // BLK
    values = filtered.astype(jnp.float32)
    prefix = jnp.concatenate(
        [jnp.zeros((station_count, 1), jnp.float32), jnp.cumsum(values * values, axis=1)], axis=1
    )
    energy = prefix[:, templ_len : templ_len + corr_len] - prefix[:, :corr_len]
    root_energy = jnp.sqrt(energy)
    hankel_rows = hankel(filtered)
    templ_norm = jnp.sqrt(jnp.sum(jnp.square(templates.astype(jnp.float32)), axis=-1) + epsilon)
    lag_index = jnp.arange(out_len, dtype=jnp.int32)
    own_rows = block_rows // lax.axis_size("sta")
    templ_split = templates.reshape(block_rows, station_count, lag_blocks, BLK)
    products = jnp.zeros((station_count, block_rows, time_blocks, BLK), jnp.float32)
    for offset in range(lag_blocks):
        products = products + jnp.einsum(
            "ksb,scbd->skcd",
            templ_split[:, :, offset, :],
            hankel_rows[:, offset : offset + time_blocks],
            preferred_element_type=jnp.float32,
        )
    products = products.reshape(station_count, block_rows, corr_len)
    correlation = products / (templ_norm.T[:, :, None] * root_energy[:, None, :])
    shifts = moveout.T
    weights = presence.T.astype(jnp.float32)
    positions = shifts[:, :, None] + lag_index[None, None, :]
    aligned = jnp.take_along_axis(correlation, positions, axis=2)
    summed = lax.psum(jnp.sum(weights[:, :, None] * aligned, axis=0), "sta")
    dev_index = lax.axis_index("sta")
    stacked = lax.dynamic_slice_in_dim(summed, dev_index * own_rows, own_rows, 0)
    return stacked[None]


def solution(mesh):
    placed = (P("sta", "tpl"), P(), P("tpl", "sta", None), P("tpl", "sta"), P("tpl", "sta"))
    return jax.shard_map(
        shards, mesh=mesh, in_specs=placed, out_specs=P("tpl", "sta", None), check_vma=False
    )
```

profile of v0, /device:TPU:6, one launch (start us, length us, event | category | flops | bytes accessed | tf_op | source)
XLA Modules:
  0.0 1396.6 jit_solution(3931908676046544148)
XLA Ops:
  6.5 6.8 all_gather.3
  13.6 0.1 copy.74
  13.7 0.8 rev.3
  14.5 0.1 copy.75
  14.6 15.2 %fusion.20 = bf16[16,200,1]{0,2,1:T(2,128)(2,1)S(1)} fusion(f32[1,16,263]{1,0,2:T(1,128)S(1)} %copy.74, f32[1,1,64]{1,0,2:T(1,128)S(1)} %copy.75), kind=kOutput, calls=%fused_computation.54 | convolution fusion | flops 2457600 | bytes 23488 | tf_op jit(solution)/shard_map/conv_general_dilated | solution.py:12
  30.0 0.1 reshape.63
  30.1 0.7 copy.79
  30.9 1.2 multiply_reduce_fusion
  32.1 0.1 tile.4
  32.2 2.2 tile.10
  34.5 2.1 slice.110
  36.6 6.0 reshape.53
  42.6 1.4 fusion.18
  44.0 0.6 reduce-window.6
  44.6 0.2 slice_reduce_fusion
  44.7 0.2 reduce-window.9
  45.1 0.9 sqrt_bitcast_fusion
  46.0 0.2 fusion.2
  46.3 0.3 fusion.13
  46.6 0.3 convolution_add_fusion.6
  46.9 0.3 convolution_add_fusion.5
  47.2 0.3 convolution_add_fusion.4
  47.6 0.3 convolution_add_fusion.3
  47.9 0.3 convolution_add_fusion.2
  48.2 0.3 convolution_add_fusion.1
  48.5 0.3 convolution_add_fusion
  48.7 0.2 bitcast_divide_fusion
  49.0 787.1 %gather_fusion = f32[98304]{0:T(1024)S(1)} fusion(f32[2,128,512]{1,2,0:T(8,128)S(1)} %bitcast_divide_fusion, s32[98304]{0:T(1024)S(1)} %reshape.72), kind=kCustom, calls=%fused_computation | custom fusion | bytes 1966080 | tf_op jit(solution)/shard_map/jit(take_along_axis)/gather | solution.py:68
  836.1 0.1 reshape.75
  836.2 0.9 multiply_reduce_fusion.1
  837.1 551.3 %all-reduce.4.cloned.1.call-done = f32[128,384]{1,0:T(8,128)} async-done(((f32[128,384]{1,0:T(8,128)}), f32[128,384]{1,0:T(8,128)}) %all-reduce.4.cloned.1.call-update) | async-done | bytes 196624 | tf_op jit(solution)/shard_map/psum | solution.py:69
  1388.4 1.3 dynamic-slice_bitcast_fusion
  (39 shorter events, 0.8 us)
Async XLA Ops:
  6.5 1381.9 %all-reduce.4.cloned.1.call-start = ((), (), s32[]{:S(2)}) async-start(), calls=%async_computation | async-start | bytes 393216 | tf_op jit(solution)/shard_map/psum | solution.py:69
  14.6 15.3 %copy-start.7 = (pred[16,200,1]{1,0,2:T(8,128)(4,1)S(1)}, pred[16,200,1]{1,0,2:T(8,128)(4,1)}, u32[]{:S(2)}) copy-start(pred[16,200,1]{1,0,2:T(8,128)(4,1)} %constant.49) | copy-start | bytes 9604
  14.6 15.5 %copy-start = (bf16[128,2,1024]{2,1,0:T(2,128)(2,1)S(1)}, bf16[128,2,1024]{2,1,0:T(2,128)(2,1)}, u32[]{:S(2)}) copy-start(bf16[128,2,1024]{2,1,0:T(2,128)(2,1)} %param.7) | copy-start | bytes 1572868
  42.6 3.4 copy-start.6
  44.0 2.6 copy-start.5
  44.0 2.9 copy-start.4
  46.3 1.0 copy-start.3
  46.6 1.0 copy-start.2
  46.9 1.0 copy-start.1
  49.0 787.2 %copy-start.8 = (s32[128,2]{0,1:T(2,128)S(1)}, s32[128,2]{0,1:T(2,128)}, u32[]{:S(2)}) copy-start(s32[128,2]{0,1:T(2,128)} %param.8) | copy-start | bytes 3076
Sparse Core Ops, SparseCore 0:
  837.3 551.1 all-reduce.3
where the time goes:
time: 1400 us
  local copies, waits for them, and re-layouts  803 us (57%)
  waiting for transfers between devices  551 us (39%)
  matrix products  17.5 us (1%)
    gather x3, local copies, waits for them, and re-layouts, shards(): aligned = jnp.take_along_axis(correlation, positions, axis=2)  787 us
    psum x1, waiting for transfers between devices, shards(): summed = lax.psum(jnp.sum(weights[:, :, None] * aligned, axis=0), 'sta')  551 us
  transfers between devices with their start and end apart: 1, of which 1 were waited for; matrix products, arithmetic and copies ran while one was open for 0% of the time, Pallas kernels for 0%

commit v1 on v0

--- a/solution.py
+++ b/solution.py
@@ -6,6 +6,11 @@
 BLK = 128
 SHIFT_MOST = 128
 epsilon = 1e-06
+
+
+def gather_and_add(array, axis):
+    parts = lax.all_gather(array, axis)
+    return jnp.sum(parts, axis=0)
 
 
 def fir_apply(extended, coeffs):
@@ -66,7 +71,7 @@
     weights = presence.T.astype(jnp.float32)
     positions = shifts[:, :, None] + lag_index[None, None, :]
     aligned = jnp.take_along_axis(correlation, positions, axis=2)
-    summed = lax.psum(jnp.sum(weights[:, :, None] * aligned, axis=0), "sta")
+    summed = gather_and_add(jnp.sum(weights[:, :, None] * aligned, axis=0), "sta")
     dev_index = lax.axis_index("sta")
     stacked = lax.dynamic_slice_in_dim(summed, dev_index * own_rows, own_rows, 0)
     return stacked[None]

time: 1400 us -> 1180 us (0.84)
  waiting for transfers between devices: 551 us -> 323 us
    psum x1 -> x0, waiting for transfers between devices: 551 us -> none  [shards(): summed = lax.psum(jnp.sum(weights[:, :, None] * aligned, axis=0), 'sta')]
    all_gather x0 -> x1, waiting for transfers between devices: none -> 323 us  [gather_and_add(): parts = lax.all_gather(array, axis)]
where the time goes in v1:
time: 1180 us
  local copies, waits for them, and re-layouts  802 us (68%)
  waiting for transfers between devices  323 us (27%)
  matrix products  22.2 us (2%)
  between operations  13.6 us (1%)
    gather x3, local copies, waits for them, and re-layouts, shards(): aligned = jnp.take_along_axis(correlation, positions, axis=2)  787 us
    all_gather x1, waiting for transfers between devices, gather_and_add(): parts = lax.all_gather(array, axis)  323 us
  transfers between devices with their start and end apart: 1, of which 1 were waited for; matrix products, arithmetic and copies ran while one was open for 0% of the time, Pallas kernels for 0%

profile of v1, /device:TPU:6, one launch (start us, length us, event | category | flops | bytes accessed | tf_op | source)
XLA Modules:
  0.0 1177.4 jit_solution(12378571498583046298)
XLA Ops:
  6.5 6.9 all_gather.9
  13.8 0.1 copy.74
  13.9 0.8 rev.3
  14.6 0.1 copy.75
  14.7 15.2 %fusion.20 = bf16[16,200,1]{0,2,1:T(2,128)(2,1)S(1)} fusion(f32[1,16,263]{1,0,2:T(1,128)S(1)} %copy.74, f32[1,1,64]{1,0,2:T(1,128)S(1)} %copy.75), kind=kOutput, calls=%fused_computation.54 | convolution fusion | flops 2457600 | bytes 23488 | tf_op jit(solution)/shard_map/conv_general_dilated | solution.py:17
  30.1 0.1 reshape.63
  30.2 0.7 copy.79
  31.0 1.2 multiply_reduce_fusion
  32.2 0.1 tile.4
  32.4 2.2 tile.10
  34.6 2.1 slice.110
  36.7 6.0 reshape.53
  42.7 1.4 fusion.18
  44.1 0.6 reduce-window.6
  44.7 0.2 slice_reduce_fusion
  44.8 0.2 reduce-window.9
  45.2 0.9 sqrt_bitcast_fusion
  46.1 0.2 fusion.2
  46.4 0.3 fusion.13
  46.7 1.2 convolution_add_fusion.6
  47.9 1.2 convolution_add_fusion.5
  49.2 1.2 convolution_add_fusion.4
  50.4 1.2 convolution_add_fusion.3
  51.6 1.2 convolution_add_fusion.2
  52.9 0.3 convolution_add_fusion.1
  53.2 0.3 convolution_add_fusion
  53.5 0.2 bitcast_divide_fusion
  53.7 787.1 %gather_fusion = f32[98304]{0:T(1024)S(1)} fusion(f32[2,128,512]{1,2,0:T(8,128)S(1)} %bitcast_divide_fusion, s32[98304]{0:T(1024)S(1)} %reshape.72), kind=kCustom, calls=%fused_computation | custom fusion | bytes 1966080 | tf_op jit(solution)/shard_map/jit(take_along_axis)/gather | solution.py:73
  840.9 0.9 multiply_reduce_fusion.1
  841.9 322.9 %all-gather.3.cloned.1.call-done = f32[8192,384]{1,0:T(8,128)} async-done(((f32[128,384]{1,0:T(8,128)}), f32[8192,384]{1,0:T(8,128)}) %all-gather.3.cloned.1.call-update) | async-done | bytes 12582928 | tf_op jit(solution)/shard_map/all_gather | solution.py:12
  1164.8 5.2 reduce_sum.29
  1169.9 0.6 dynamic-slice_bitcast_fusion
  (30 shorter events, 0.8 us)
Async XLA Ops:
  6.5 23.5 %copy-start.2 = (pred[16,200,1]{1,0,2:T(8,128)(4,1)S(1)}, pred[16,200,1]{1,0,2:T(8,128)(4,1)}, u32[]{:S(2)}) copy-start(pred[16,200,1]{1,0,2:T(8,128)(4,1)} %constant.49) | copy-start | bytes 9604
  6.5 23.7 %copy-start = (bf16[128,2,1024]{2,1,0:T(2,128)(2,1)S(1)}, bf16[128,2,1024]{2,1,0:T(2,128)(2,1)}, u32[]{:S(2)}) copy-start(bf16[128,2,1024]{2,1,0:T(2,128)(2,1)} %param.7) | copy-start | bytes 1572868
  6.5 1158.2 %all-gather.3.cloned.1.call-start = ((), (), s32[]{:S(2)}) async-start(), calls=%async_computation | async-start | bytes 12779520 | tf_op jit(solution)/shard_map/all_gather | solution.py:12
  30.0 16.2 %copy-start.1 = (s32[128,2]{0,1:T(2,128)S(1)}, s32[128,2]{0,1:T(2,128)}, u32[]{:S(2)}) copy-start(s32[128,2]{0,1:T(2,128)} %param.9) | copy-start | bytes 3076
  53.7 787.2 %copy-start.3 = (s32[128,2]{0,1:T(2,128)S(1)}, s32[128,2]{0,1:T(2,128)}, u32[]{:S(2)}) copy-start(s32[128,2]{0,1:T(2,128)} %param.8) | copy-start | bytes 3076
Sparse Core Ops, SparseCore 0:
  842.0 322.7 all-gather.2
